TPU v7x, 32 devices: a whole 2x2x4 slice. The times are simulated.
32 devices in a mesh: groups: 2 (over y), row: 16 (over z, x, core).
Axes of the slice: x: 2, y: 2, z: 4, core: 2. Of those that a mesh axis runs over, the one named last changes fastest.
Arguments:
- object_tiles: bfloat16 [8192, 2, 2048], P(('groups', 'row')), parts along dimension 0, may hold values from -4 to 4
- probe: float32 [4, 256, 2, 256], replicated, may hold values from -3 to 3
- measured: bfloat16 [192, 256, 256], P(('groups', 'row')), parts along dimension 0, may hold values from 0.19921875 to 2.5
- offset_row: int32 [192], P(('groups', 'row')), parts along dimension 0, may hold values from 0 to 255
- offset_col: int32 [192], P(('groups', 'row')), parts along dimension 0, may hold values from 0 to 1791
- subpixel: int32 [192], P(('groups', 'row')), parts along dimension 0, may hold values from 0 to 15
- live_count: int32 [32], P(('groups', 'row')), parts along dimension 0, may hold values from 1 to 6, 48 in all
Outputs:
- object_grad: float32 [8192, 2, 2048], P(('groups', 'row')), parts along dimension 0
- probe_grad: float32 [8, 256, 2, 256], P('groups'), parts along dimension 0
- position_grad: float32 [2, 192], P(None, ('groups', 'row')), parts along dimension 1
There are 2 independent parts, one for each index of `groups`. A program takes and returns all parts, laid end to end along the dimension named above; an argument that names none is the same for every part. Nothing has to cross between parts.
Inputs may be any that keep to these rules, and one draw needn't show every extreme that they name: Device d's live slots are its first live_count[d] slots; live_count sums to 48 and reaches 6 on some device.
All inputs are finite; a program needn't handle non-finite values.
Results may differ from a plain program's by a relative error of at most 0.0099.
Values may be sent and summed in bfloat16 or wider, within the bound.
A program may use at most 128 MiB of HBM per device.

v0:
```python
import math

import jax
import jax.numpy as jnp
from jax import lax
from jax.sharding import PartitionSpec as P


def passed_along(x, axis, by):
    length = lax.axis_size(axis)
    pairs = [(i, i + by) for i in range(length) if 0 <= i + by < length]
    return lax.ppermute(x, axis, pairs)


def dft_tables(patch):
    index = jnp.arange(patch, dtype=jnp.int32)
    phase = index[:, None] * index[None, :] % patch
    angle = phase.astype(jnp.float32) * (2.0 * math.pi / patch)
    scale = 1.0 / math.sqrt(patch)
    cosine = (jnp.cos(angle) * scale).astype(jnp.bfloat16)
    sine = (jnp.sin(angle) * scale).astype(jnp.bfloat16)
    along_x = jnp.concatenate(
        [jnp.concatenate([cosine, -sine], 1), jnp.concatenate([sine, cosine], 1)], 0
    )
    along_y = jnp.concatenate(
        [
            jnp.stack([cosine, sine], -1).reshape(patch, 2 * patch),
            jnp.stack([-sine, cosine], -1).reshape(patch, 2 * patch),
        ],
        0,
    )
    inverse_y = jnp.stack(
        [jnp.concatenate([cosine, -sine], 1), jnp.concatenate([sine, cosine], 1)], 1
    ).reshape(2 * patch, 2 * patch)
    inverse_x = jnp.concatenate(
        [jnp.concatenate([cosine, sine], 1), jnp.concatenate([-sine, cosine], 1)], 0
    )
    return (along_x, along_y, inverse_y, inverse_x)


def fractions(code):
    return ((code // 4).astype(jnp.float32) * 0.25, (code % 4).astype(jnp.float32) * 0.25)


def interpolate(window, code):
    frac_y, frac_x = fractions(code)
    cells = window.astype(jnp.float32)
    size = cells.shape[0] - 1
    upper = (1.0 - frac_x) * cells[:size, :, :size] + frac_x * cells[:size, :, 1:]
    lower = (1.0 - frac_x) * cells[1:, :, :size] + frac_x * cells[1:, :, 1:]
    return (1.0 - frac_y) * upper + frac_y * lower


def spread(grad_patch, frac_y, frac_x):

    def sideways(part):
        return jnp.pad((1.0 - frac_x) * part, ((0, 0), (0, 0), (0, 1))) + jnp.pad(
            frac_x * part, ((0, 0), (0, 0), (1, 0))
        )

    upper = sideways((1.0 - frac_y) * grad_patch)
    lower = sideways(frac_y * grad_patch)
    return jnp.pad(upper, ((0, 1), (0, 0), (0, 0))) + jnp.pad(lower, ((1, 0), (0, 0), (0, 0)))


def slopes(window, grad_patch, frac_y, frac_x):
    cells = window.astype(jnp.float32)
    size = cells.shape[0] - 1
    down = cells[1:] - cells[:size]
    slope_y = (1.0 - frac_x) * down[:, :, :size] + frac_x * down[:, :, 1:]
    across = cells[:, :, 1:] - cells[:, :, :size]
    slope_x = (1.0 - frac_y) * across[:size] + frac_y * across[1:]
    return (jnp.sum(grad_patch * slope_y) / size, jnp.sum(grad_patch * slope_x) / size)


def project(patch_obj, amplitude, probe, tables):
    along_x, along_y, inverse_y, inverse_x = tables
    modes = probe.shape[0]
    size = probe.shape[1]
    preal = probe[:, :, 0, :]
    pimag = probe[:, :, 1, :]
    oreal = patch_obj[:, 0, :]
    oimag = patch_obj[:, 1, :]
    wave = jnp.stack([preal * oreal - pimag * oimag, preal * oimag + pimag * oreal], axis=2).astype(
        jnp.bfloat16
    )
    first = jnp.dot(
        wave.reshape(modes * size, 2 * size), along_x, preferred_element_type=jnp.float32
    ).astype(jnp.bfloat16)
    far = jnp.einsum(
        "ab,mbk->mak",
        along_y,
        first.reshape(modes, 2 * size, size),
        preferred_element_type=jnp.float32,
    )
    far = far.reshape(modes, 2, size, size)
    modulus = jnp.maximum(jnp.sqrt(jnp.sum(far * far, axis=(0, 1))), 0.5)
    ratio = 1.0 - amplitude.astype(jnp.float32) / modulus
    error = (far * ratio).astype(jnp.bfloat16)
    back = jnp.einsum(
        "ab,mbk->mak",
        inverse_y,
        error.reshape(modes, 2 * size, size),
        preferred_element_type=jnp.float32,
    ).astype(jnp.bfloat16)
    exit_grad = jnp.dot(
        back.reshape(modes * size, 2 * size), inverse_x, preferred_element_type=jnp.float32
    ).reshape(modes, size, 2, size)
    ureal = exit_grad[:, :, 0, :]
    uimag = exit_grad[:, :, 1, :]
    obj_grad = jnp.stack(
        [jnp.sum(preal * ureal + pimag * uimag, 0), jnp.sum(preal * uimag - pimag * ureal, 0)],
        axis=1,
    )
    probe_term = jnp.stack([oreal * ureal + oimag * uimag, oreal * uimag - oimag * ureal], axis=2)
    return (obj_grad, probe_term)


def shards(object_tiles, probe, measured, offset_row, offset_col, subpixel, live_count):
    rows = object_tiles.shape[0]
    width = object_tiles.shape[2]
    size = probe.shape[1]
    slots = measured.shape[0]
    spare = slots // 2
    tables = dft_tables(size)
    count = live_count[0]
    slot_ids = jnp.arange(slots, dtype=jnp.int32)
    rim = passed_along(object_tiles, "row", -1)
    extended = jnp.concatenate([object_tiles, rim], axis=0)

    def cut(index):
        return lax.dynamic_slice(
            extended, (offset_row[index], 0, offset_col[index]), (size + 1, 2, size + 1)
        )

    windows = lax.map(cut, slot_ids)
    empty_grads = jnp.zeros((slots + spare, size, 2, size), jnp.float32)
    empty_probe = jnp.zeros(probe.shape, jnp.float32)

    def own_slot(index, carry):
        grads, probe_acc = carry
        patch_obj = interpolate(windows[index], subpixel[index])
        obj_grad, probe_term = project(patch_obj, measured[index], probe, tables)
        return (grads.at[index].set(obj_grad), probe_acc + probe_term)

    grads, probe_acc = lax.fori_loop(0, count, own_slot, (empty_grads, empty_probe))
    probe_grad = lax.psum(probe_acc, "row")

    def settle(index, carry):
        grad_ext, moved = carry
        frac_y, frac_x = fractions(subpixel[index])
        obj_grad = grads[index]
        corner = (offset_row[index], 0, offset_col[index])
        region = lax.dynamic_slice(grad_ext, corner, (size + 1, 2, size + 1))
        grad_ext = lax.dynamic_update_slice(
            grad_ext, region + spread(obj_grad, frac_y, frac_x), corner
        )
        slope_y, slope_x = slopes(windows[index], obj_grad, frac_y, frac_x)
        moved = moved.at[:, index].set(jnp.stack([slope_y, slope_x]))
        return (grad_ext, moved)

    start = (jnp.zeros((rows + size, 2, width), jnp.float32), jnp.zeros((2, slots), jnp.float32))
    grad_ext, moved = lax.fori_loop(0, count, settle, start)
    own_rows = grad_ext[:rows]
    below = passed_along(grad_ext[rows:], "row", 1)
    object_grad = own_rows.at[:size].add(below)
    return (object_grad, probe_grad, moved)


def solution(mesh):
    in_specs = (
        P(("groups", "row"), None, None),
        P(),
        P(("groups", "row"), None, None),
        P(("groups", "row")),
        P(("groups", "row")),
        P(("groups", "row")),
        P(("groups", "row")),
    )
    out_specs = (
        P(("groups", "row"), None, None),
        P("groups", None, None, None),
        P(None, ("groups", "row")),
    )
    return jax.shard_map(shards, mesh=mesh, in_specs=in_specs, out_specs=out_specs, check_vma=False)
```

profile of v0, /device:TPU:0, one launch (start us, length us, event | category | flops | bytes accessed | tf_op | source)
XLA Modules:
  0.0 840.9 jit_solution(12319592840080099803)
XLA Ops:
  18.2 9.6 %pad_maximum_fusion.1 = bf16[512,2,2048]{2,1,0:T(2,128)(2,1)} fusion(bf16[256,2,2048]{2,1,0:T(2,128)(2,1)} %collective-permute-done, bf16[256,2,2048]{2,1,0:T(2,128)(2,1)} %param.21), kind=kLoop, calls=%fused_computation.72 | loop fusion | flops 2097152 | bytes 8388608 | tf_op jit(solution)/shard_map/concatenate | solution.py:129
  27.8 56.7 %while.42 = (s32[]{:T(128)}, bf16[6,257,2,257]{3,2,1,0:T(2,128)(2,1)}, s32[6]{0:T(128)S(1)}, s32[6]{0:T(128)S(1)}, s32[6]{0:T(128)S(1)}, /*index=5*/bf16[512,2,2...) while((s32[]{:T(128)}, bf16[6,257,2,257]{3,2,1,0:T(2,128)(2,1)}, ...), condition=%wide.region_1.2_spmd, body=%wide.region_0.1_spmd.sunk | while | flops 11 | bytes 789771 | solution.py:136
  34.6 2.6 bitcast_dynamic-update-slice_fusion.2
  44.1 2.6 bitcast_dynamic-update-slice_fusion.2
  53.5 2.6 bitcast_dynamic-update-slice_fusion.2
  62.9 2.6 bitcast_dynamic-update-slice_fusion.2
  72.3 2.6 bitcast_dynamic-update-slice_fusion.2
  81.7 2.6 bitcast_dynamic-update-slice_fusion.2
  86.0 3.6 broadcast_in_dim.22
  89.6 64.7 %while.43 = (s32[]{:T(128)}, f32[9,256,2,256]{3,2,1,0:T(2,128)}, f32[4,256,2,256]{3,1,2,0:T(8,128)}, s32[]{:T(128)}, f32[4,256,2,256]{3,1,2,0:T(8,128)S(1)}, /*i...) while((s32[]{:T(128)}, f32[9,256,2,256]{3,2,1,0:T(2,128)}, ...), condition=%wide.region_8.9_spmd, body=%wide.region_2.8_spmd.sunk | while | flops 2159608832 | bytes 92680056 | solution.py:146
  102.3 4.0 fusion.77
  109.9 1.8 fusion.79
  114.4 1.8 fusion.80
  118.4 3.1 fusion.81
  134.2 4.0 fusion.77
  141.8 1.8 fusion.79
  146.3 1.8 fusion.80
  150.3 3.1 fusion.81
  154.3 7.5 broadcast_in_dim.21
  161.8 136.3 %while.44 = (s32[]{:T(128)}, f32[512,2,2048]{2,1,0:T(2,128)}, f32[2,6]{0,1:T(8,128)S(1)}, s32[]{:T(128)}, s32[6]{0:T(128)S(1)}, /*index=5*/s32[6]{0:T(128)S(1)},...) while((s32[]{:T(128)}, f32[512,2,2048]{2,1,0:T(2,128)}, ...), condition=%wide.region_13.14_spmd, body=%wide.region_9.13_spmd.sunk | while | flops 3019835 | bytes 15514405 | solution.py:163
  173.5 3.0 fusion.84
  180.0 2.2 add_add_fusion.2
  182.2 47.5 %dynamic_update_slice.14 = f32[512,2,2048]{2,1,0:T(2,128)} dynamic-update-slice(f32[512,2,2048]{2,1,0:T(2,128)} %get-tuple-element.846, f32[257,2,257]{2,1,0:T(2,128)S(1)} %add_add_fusion.2, s32[]{:T(128)S(6)} %select_n.184, s32[]{:T(128)} %constant.305.clone.1..sunk.2, s32[]{:T(128)S(6)} %select_n.185) | dynamic-update-slice | bytes 1056788 | tf_op jit(solution)/shard_map/while/body/dynamic_update_slice | solution.py:155
  241.4 3.0 fusion.84
  247.8 2.2 add_add_fusion.2
  250.0 47.5 %dynamic_update_slice.14 = f32[512,2,2048]{2,1,0:T(2,128)} dynamic-update-slice(f32[512,2,2048]{2,1,0:T(2,128)} %get-tuple-element.846, f32[257,2,257]{2,1,0:T(2,128)S(1)} %add_add_fusion.2, s32[]{:T(128)S(6)} %select_n.184, s32[]{:T(128)} %constant.305.clone.1..sunk.2, s32[]{:T(128)S(6)} %select_n.185) | dynamic-update-slice | bytes 1056788 | tf_op jit(solution)/shard_map/while/body/dynamic_update_slice | solution.py:155
  298.2 6.3 slice.174
  304.5 121.9 %collective-permute-start.1 = (f32[256,2,2048]{2,1,0:T(2,128)}, f32[256,2,2048]{2,1,0:T(2,128)}, u32[]{:S(2)}, u32[]{:S(2)}) collective-permute-start(f32[256,2,2048]{2,1,0:T(2,128)} %slice.174), channel_id=1, source_target_pairs={{0,1},{1,2},{2,3},{3,4},{4,5},{5,6},{6,7},{7,8},{8,9},{9,10},{10,1... | collective-permute-start | bytes 12582920 | tf_op jit(solution)/shard_map/ppermute | solution.py:12
  426.3 2.9 copy.50
  431.2 9.5 %slice_add_fusion = f32[256,2,2048]{2,1,0:T(2,128)} fusion(f32[256,2,2048]{2,1,0:T(2,128)} %collective-permute-done.1, f32[512,2,2048]{2,1,0:T(2,128)} %get-tuple-element.358), kind=kLoop, calls=%fused_computation.73 | loop fusion | flops 1048576 | bytes 12582912 | tf_op jit(solution)/shard_map/add | solution.py:166
  440.7 389.3 %all-reduce.8.cloned.1.call-done = f32[4,256,2,256]{3,2,1,0:T(2,128)} async-done(((f32[4,256,2,256]{3,2,1,0:T(2,128)}), f32[4,256,2,256]{3,2,1,0:T(2,128)}) %all-reduce.8.cloned.1.call-update) | async-done | bytes 2097168 | tf_op jit(solution)/shard_map/psum | solution.py:147
  830.0 3.6 copy.102
  (162 shorter events, 74.4 us)
Async XLA Ops:
  7.2 822.8 %all-reduce.8.cloned.1.call-start = ((), (), s32[]{:S(2)}) async-start(), calls=%async_computation | async-start | bytes 4194304 | tf_op jit(solution)/shard_map/psum | solution.py:147
  7.2 11.0 %collective-permute-start = (bf16[256,2,2048]{2,1,0:T(2,128)(2,1)}, bf16[256,2,2048]{2,1,0:T(2,128)(2,1)}, u32[]{:S(2)}, u32[]{:S(2)}) collective-permute-start(bf16[256,2,2048]{2,1,0:T(2,128)(2,1)} %param.21), channel_id=1, source_target_pairs={{1,0},{2,1},{3,2},{4,3},{5,4},{6,5},{7,6},{8,7},{9,8},{10,9},{11,1... | collective-permute-start | bytes 6291464 | tf_op jit(solution)/shard_map/ppermute | solution.py:12
  18.1 9.7 %copy-start.11 = (s32[6]{0:T(128)S(1)}, s32[6]{0:T(128)}, u32[]{:S(2)}) copy-start(s32[6]{0:T(128)} %param.24) | copy-start | bytes 76
  18.2 9.7 %copy-start.12 = (s32[6]{0:T(128)S(1)}, s32[6]{0:T(128)}, u32[]{:S(2)}) copy-start(s32[6]{0:T(128)} %param.25) | copy-start | bytes 76
  86.0 3.7 copy-start.10
  86.0 3.7 copy-start.13
  90.3 6.5 copy-start.6
  90.3 8.9 %copy-start.8 = (bf16[512,512]{1,0:T(8,128)(2,1)}, bf16[512,512]{1,0:T(8,128)(2,1)S(1)}, u32[]{:S(2)}) copy-start(bf16[512,512]{1,0:T(8,128)(2,1)S(1)} %get-tuple-element.804) | copy-start | bytes 1572868 | tf_op jit(solution)/shard_map/while
  97.2 0.7 copy-start.4
  108.3 1.6 copy-start
  114.4 1.8 copy-start.5
  116.3 1.6 copy-start.1
  117.9 3.7 copy-start.7
  117.9 3.7 copy-start.9
  118.4 3.2 copy-start.2
  122.2 6.5 copy-start.6
  122.2 8.9 %copy-start.8 = (bf16[512,512]{1,0:T(8,128)(2,1)}, bf16[512,512]{1,0:T(8,128)(2,1)S(1)}, u32[]{:S(2)}) copy-start(bf16[512,512]{1,0:T(8,128)(2,1)S(1)} %get-tuple-element.804) | copy-start | bytes 1572868 | tf_op jit(solution)/shard_map/while
  129.1 0.7 copy-start.4
  140.2 1.6 copy-start
  146.3 1.8 copy-start.5
  148.2 1.6 copy-start.1
  149.8 3.7 copy-start.7
  149.8 3.7 copy-start.9
  150.3 3.2 copy-start.2
  298.2 128.1 %copy-start.3 = (f32[4,256,2,256]{3,1,2,0:T(8,128)S(1)}, f32[4,256,2,256]{3,1,2,0:T(8,128)}, u32[]{:S(2)}) copy-start(f32[4,256,2,256]{3,1,2,0:T(8,128)} %get-tuple-element.359) | copy-start | bytes 6291460
  304.5 126.8 %collective-permute-start.1 = (f32[256,2,2048]{2,1,0:T(2,128)}, f32[256,2,2048]{2,1,0:T(2,128)}, u32[]{:S(2)}, u32[]{:S(2)}) collective-permute-start(f32[256,2,2048]{2,1,0:T(2,128)} %slice.174), channel_id=1, source_target_pairs={{0,1},{1,2},{2,3},{3,4},{4,5},{5,6},{6,7},{7,8},{8,9},{9,10},{10,1... | collective-permute-start | bytes 12582920 | tf_op jit(solution)/shard_map/ppermute | solution.py:12
Sparse Core Ops, SparseCore 0:
  429.4 400.5 all-reduce.7
where the time goes:
time: 854 us; the launch traced here: 841 us
  waiting for transfers between devices  391 us (46%)
  local copies, waits for them, and re-layouts  181 us (21%)
  starting transfers between devices  123 us (14%)
  other arithmetic  57.7 us (7%)
  loops' own time  55 us (6%)
  matrix products  18.5 us (2%)
  between operations  14.7 us (2%)
    psum x1, waiting for transfers between devices, shards(): probe_grad = lax.psum(probe_acc, 'row')  389 us
    ppermute x2, starting transfers between devices, passed_along(): return lax.ppermute(x, axis, pairs)  123 us
    dynamic_update_slice x2, local copies, waits for them, and re-layouts, settle(): lax.dynamic_update_slice(grad_ext, region + spread(obj_grad, frac_y, frac...  95 us
    another operation x1, loops' own time, shards(): windows = lax.map(cut, slot_ids)  30.5 us
  transfers between devices with their start and end apart: 3, of which 2 were waited for; matrix products, arithmetic and copies ran while one was open for 3% of the time, Pallas kernels for 0%

commit v1 on v0

v1 whole, which is shorter than its diff:
```python
import functools
import math

import jax
import jax.numpy as jnp
import numpy as np
from jax import lax
from jax.experimental import pallas as pl
from jax.experimental.pallas import tpu as pltpu
from jax.sharding import PartitionSpec as P

LANES = 128
ROWS = 16


def passed_along(x, axis, by):
    length = lax.axis_size(axis)
    pairs = [(i, i + by) for i in range(length) if 0 <= i + by < length]
    return lax.ppermute(x, axis, pairs)


def summed(x, axis):
    length = lax.axis_size(axis)
    lines = x.size // x.shape[-1]
    if length & (length - 1) or lines % (length * ROWS):
        return lax.psum(x, axis)
    me = lax.axis_index(axis)
    part = x.reshape(length, lines // length, x.shape[-1])
    steps = [1 << k for k in range(length.bit_length() - 1)]

    def swap(y, step):
        return lax.ppermute(y, axis, [(i, i ^ step) for i in range(length)])

    for step in steps:
        many = part.shape[0] // 2
        bit = (me // step) % 2
        kept = lax.dynamic_slice_in_dim(part, bit * many, many, 0)
        sent = lax.dynamic_slice_in_dim(part, (1 - bit) * many, many, 0)
        part = kept + swap(sent.astype(jnp.bfloat16), step).astype(jnp.float32)
    part = part.astype(jnp.bfloat16)
    for step in reversed(steps):
        bit = (me // step) % 2
        other = swap(part, step)
        part = jnp.where(
            bit == 0, jnp.concatenate([part, other], 0), jnp.concatenate([other, part], 0)
        )
    return part.reshape(x.shape).astype(jnp.float32)


def dft_tables(patch):
    index = np.arange(patch)
    angle = ((index[:, None] * index[None, :]) % patch).astype(np.float64) * (2.0 * math.pi / patch)
    scale = 1.0 / math.sqrt(patch)
    cosine = jnp.asarray((np.cos(angle) * scale).astype(np.float32)).astype(jnp.bfloat16)
    sine = jnp.asarray((np.sin(angle) * scale).astype(np.float32)).astype(jnp.bfloat16)
    return cosine, sine


def pulled(x, by, tiles):
    lane = lax.broadcasted_iota(jnp.int32, x[0].shape, 1)
    back = lax.rem(LANES - by, LANES)
    parts = [pltpu.roll(x[k], back, 1) for k in range(tiles + 1)]
    keep = lane < LANES - by
    return [jnp.where(keep, parts[k], parts[k + 1]) for k in range(tiles)]


def pushed(x, by, tiles):
    lane = lax.broadcasted_iota(jnp.int32, (x.shape[0], LANES), 1)
    ahead = lax.rem(by, LANES)
    parts = [pltpu.roll(x[:, k * LANES : (k + 1) * LANES], ahead, 1) for k in range(tiles)]
    zero = jnp.zeros_like(parts[0])
    keep = lane >= by
    left = [zero] + parts
    right = parts + [zero]
    return [jnp.where(keep, right[k], left[k]) for k in range(tiles + 1)]


def step_kernel(
    modes, size, rows,
    count_ref, top_ref, left_ref, code_ref,
    own_hbm, rim_hbm, probe_ref, measured_ref, cos_ref, sin_ref,
    grad_ref, below_ref, pgrad_ref, moved_ref,
    ext, win, acc, table_a, table_b, patch, slope, far, power, gsum, sems,
):
    f32, bf16 = jnp.float32, jnp.bfloat16
    tiles = size // LANES
    slots = measured_ref.shape[0]
    wide = size + LANES
    copies = [
        pltpu.make_async_copy(own_hbm, ext.at[:, pl.ds(0, rows), :], sems.at[0]),
        pltpu.make_async_copy(rim_hbm, ext.at[:, pl.ds(rows, size), :], sems.at[1]),
    ]
    for copy in copies:
        copy.start()
    cosine, sine = cos_ref[...], sin_ref[...]
    table_a[0:size, 0:size] = cosine
    table_a[0:size, size : 2 * size] = -sine
    table_a[size : 2 * size, 0:size] = sine
    table_a[size : 2 * size, size : 2 * size] = cosine
    table_b[0:size, 0:size] = cosine
    table_b[0:size, size : 2 * size] = sine
    table_b[size : 2 * size, 0:size] = -sine
    table_b[size : 2 * size, size : 2 * size] = cosine
    pgrad_ref[...] = jnp.zeros_like(pgrad_ref)
    span = 32

    @pl.loop(0, (rows + size) // span)
    def _(i):
        at = pl.ds(pl.multiple_of(i * span, span), span)
        acc[:, :, at, :] = jnp.zeros((2, acc.shape[1], span, LANES), f32)

    for j in range(slots):
        moved_ref[0, j] = 0.0
        moved_ref[1, j] = 0.0
    for copy in copies:
        copy.wait()

    @pl.loop(0, count_ref[0])
    def _(j):
        top, left, code = top_ref[j], left_ref[j], code_ref[j]
        base_row = pl.multiple_of(top // ROWS * ROWS, ROWS)
        row = top - base_row
        base_col = pl.multiple_of(left // LANES * LANES, LANES)
        col = left - base_col
        fy = (code // 4).astype(f32) * 0.25
        fx = (code % 4).astype(f32) * 0.25
        cols = pl.ds(base_col, wide)
        chunk = 64

        for p in range(2):
            cut = ext[p, pl.ds(base_row, size + ROWS), cols].astype(f32)
            for k in range(tiles + 1):
                win[p, k] = cut[:, k * LANES : (k + 1) * LANES]

        @pl.loop(0, size // chunk)
        def _(i):
            at = pl.multiple_of(i * chunk, chunk)
            here = pl.ds(at, chunk)
            for p in range(2):
                v, d = [], []
                for k in range(tiles + 1):
                    upper = win[p, k, pl.ds(at + row, chunk), :]
                    lower = win[p, k, pl.ds(at + row + 1, chunk), :]
                    v.append((1.0 - fy) * upper + fy * lower)
                    d.append(lower - upper)
                v0, v1 = pulled(v, col, tiles), pulled(v, col + 1, tiles)
                d0, d1 = pulled(d, col, tiles), pulled(d, col + 1, tiles)
                for k in range(tiles):
                    to = pl.ds(k * LANES, LANES)
                    patch[p, here, to] = (1.0 - fx) * v0[k] + fx * v1[k]
                    slope[0, p, here, to] = (1.0 - fx) * d0[k] + fx * d1[k]
                    slope[1, p, here, to] = v1[k] - v0[k]

        power[...] = jnp.zeros_like(power)
        gsum[...] = jnp.zeros_like(gsum)

        @pl.loop(0, modes, unroll=True)
        def _(m):
            pr, pi = probe_ref[m, 0], probe_ref[m, 1]
            re, im = patch[0], patch[1]
            wave = jnp.concatenate(
                [(pr * re - pi * im).astype(bf16), (pr * im + pi * re).astype(bf16)], axis=1
            )
            half = jnp.dot(wave, table_a[...], preferred_element_type=f32).astype(bf16)
            stacked = jnp.concatenate([half[:, :size], half[:, size:]], axis=0)
            both = jnp.dot(table_b[...], stacked, preferred_element_type=f32)
            far[m] = both
            fr, fi = both[:size], both[size:]
            power[...] += fr * fr + fi * fi

        modulus = jnp.maximum(jnp.sqrt(power[...]), 0.5)
        power[...] = 1.0 - measured_ref[j].astype(f32) / modulus

        @pl.loop(0, modes, unroll=True)
        def _(m):
            ratio = power[...]
            error = jnp.concatenate(
                [(far[m, :size] * ratio).astype(bf16), (far[m, size:] * ratio).astype(bf16)], axis=0
            )
            back = jnp.dot(table_a[...], error, preferred_element_type=f32).astype(bf16)
            side = jnp.concatenate([back[:size], back[size:]], axis=1)
            exit_grad = jnp.dot(side, table_b[...], preferred_element_type=f32)
            ur, ui = exit_grad[:, :size], exit_grad[:, size:]
            pr, pi = probe_ref[m, 0], probe_ref[m, 1]
            re, im = patch[0], patch[1]
            gsum[0] += pr * ur + pi * ui
            gsum[1] += pr * ui - pi * ur
            pgrad_ref[m, 0] += re * ur + im * ui
            pgrad_ref[m, 1] += re * ui - im * ur

        for s in range(2):
            total = jnp.sum(gsum[0] * slope[s, 0] + gsum[1] * slope[s, 1])
            moved_ref[s, j] = total / size

        @pl.loop(0, size // chunk)
        def _(i):
            at = pl.multiple_of(i * chunk, chunk)
            for p in range(2):
                g = gsum[p, pl.ds(at, chunk), :]
                s0, s1 = pushed(g, col, tiles), pushed(g, col + 1, tiles)
                for k in range(tiles + 1):
                    s = (1.0 - fx) * s0[k] + fx * s1[k]
                    tile = left // LANES + k
                    acc[p, tile, pl.ds(top + at, chunk), :] += (1.0 - fy) * s
                    acc[p, tile, pl.ds(top + at + 1, chunk), :] += fy * s

    @pl.loop(0, rows // span)
    def _(i):
        at = pl.multiple_of(i * span, span)
        for k in range(acc.shape[1]):
            grad_ref[:, pl.ds(at, span), pl.ds(k * LANES, LANES)] = acc[:, k, pl.ds(at, span), :]

    @pl.loop(0, size // span)
    def _(i):
        at = pl.multiple_of(i * span, span)
        for k in range(acc.shape[1]):
            below_ref[:, pl.ds(at, span), pl.ds(k * LANES, LANES)] = acc[
                :, k, pl.ds(rows + at, span), :
            ].astype(bf16)


def shards(object_tiles, probe, measured, offset_row, offset_col, subpixel, live_count):
    f32, bf16 = jnp.float32, jnp.bfloat16
    rows, _, width = object_tiles.shape
    modes, size = probe.shape[:2]
    slots = measured.shape[0]
    own = jnp.transpose(object_tiles, (1, 0, 2))
    rim = passed_along(own[:, :size], "row", -1)
    probe_planes = jnp.transpose(probe, (0, 2, 1, 3))
    cosine, sine = dft_tables(size)
    vmem = pl.BlockSpec(memory_space=pltpu.VMEM)
    smem = pl.BlockSpec(memory_space=pltpu.SMEM)
    hbm = pl.BlockSpec(memory_space=pl.ANY)
    grad, below, probe_sum, moved = pl.pallas_call(
        functools.partial(step_kernel, modes, size, rows),
        out_shape=(
            jax.ShapeDtypeStruct((2, rows, width), f32),
            jax.ShapeDtypeStruct((2, size, width), bf16),
            jax.ShapeDtypeStruct((modes, 2, size, size), f32),
            jax.ShapeDtypeStruct((2, slots), f32),
        ),
        in_specs=[smem] * 4 + [hbm] * 2 + [vmem] * 4,
        out_specs=(vmem, vmem, vmem, smem),
        scratch_shapes=[
            pltpu.VMEM((2, rows + size, width), bf16),
            pltpu.VMEM((2, size // LANES + 1, size + ROWS, LANES), f32),
            pltpu.VMEM((2, width // LANES, rows + size, LANES), f32),
            pltpu.VMEM((2 * size, 2 * size), bf16),
            pltpu.VMEM((2 * size, 2 * size), bf16),
            pltpu.VMEM((2, size, size), f32),
            pltpu.VMEM((2, 2, size, size), f32),
            pltpu.VMEM((modes, 2 * size, size), f32),
            pltpu.VMEM((size, size), f32),
            pltpu.VMEM((2, size, size), f32),
            pltpu.SemaphoreType.DMA((2,)),
        ],
        compiler_params=pltpu.CompilerParams(vmem_limit_bytes=60 << 20),
        name="step",
    )(live_count, offset_row, offset_col, subpixel, own, rim, probe_planes, measured, cosine, sine)
    landed = passed_along(below, "row", 1)
    probe_grad = jnp.transpose(summed(probe_sum, "row"), (0, 2, 1, 3))
    grad = grad.at[:, :size].add(landed.astype(f32))
    return (jnp.transpose(grad, (1, 0, 2)), probe_grad, moved)


def solution(mesh):
    in_specs = (
        P(("groups", "row"), None, None),
        P(),
        P(("groups", "row"), None, None),
        P(("groups", "row")),
        P(("groups", "row")),
        P(("groups", "row")),
        P(("groups", "row")),
    )
    out_specs = (
        P(("groups", "row"), None, None),
        P("groups", None, None, None),
        P(None, ("groups", "row")),
    )
    return jax.shard_map(shards, mesh=mesh, in_specs=in_specs, out_specs=out_specs, check_vma=False)
```

time: 854 us -> 144 us (0.17); the launches traced: 841 us -> 143 us
  waiting for transfers between devices: 391 us -> 36.9 us
  local copies, waits for them, and re-layouts: 181 us -> 15.1 us
  starting transfers between devices: 123 us -> 44.7 us
  other arithmetic: 57.7 us -> 2.54 us
  loops' own time: 55 us -> 0 us
  Pallas kernels: 0 us -> 42.6 us
  matrix products: 18.5 us -> 0 us
  between operations: 14.7 us -> 1.51 us
    psum x1 -> x0, waiting for transfers between devices: 389 us -> none  [shards(): probe_grad = lax.psum(probe_acc, 'row')]
    ppermute x2, starting transfers between devices: 123 us -> 3.31 us  [passed_along(): return lax.ppermute(x, axis, pairs)]
    dynamic_update_slice x8 -> x0, local copies, waits for them, and re-layouts: 111 us -> none  [the longest x2 95 us: settle(): lax.dynamic_update_slice(grad_ext, region + spread(obj_grad, frac_y, frac...]
    another operation x3 -> x0, loops' own time: 55 us -> none  [the longest x1 30.5 us: shards(): windows = lax.map(cut, slot_ids)]
    pallas_call x0 -> x1, Pallas kernels: none -> 42.6 us  [shards(): pl.pallas_call(functools.partial(step_kernel, modes, size, rows), out_sha...]
    ppermute x0 -> x8, starting transfers between devices: none -> 41.4 us  [swap(): return lax.ppermute(y, axis, [(i, i ^ step) for i in range(length)])]
    ppermute x0 -> x8, waiting for transfers between devices: none -> 35.7 us  [swap(): return lax.ppermute(y, axis, [(i, i ^ step) for i in range(length)])]
    dynamic_slice x32 -> x0, local copies, waits for them, and re-layouts: 19.9 us -> none  [the longest x4 3.93 us: own_slot(): patch_obj = interpolate(windows[index], subpixel[index])]
  transfers between devices with their start and end apart: 3 -> 10, of which waited for: 2 -> 9; matrix products, arithmetic and copies ran while one was open for 3% -> 5% of each run, Pallas kernels for 0% -> 0%
where the time goes in v1:
time: 144 us; the launch traced here: 143 us
  starting transfers between devices  44.7 us (31%)
  Pallas kernels  42.6 us (30%)
  waiting for transfers between devices  36.9 us (26%)
  local copies, waits for them, and re-layouts  15.1 us (10%)
  other arithmetic  2.54 us (2%)
  between operations  1.51 us (1%)
    pallas_call x1, Pallas kernels, shards(): pl.pallas_call(functools.partial(step_kernel, modes, size, rows), out_sha...  42.6 us
    ppermute x8, starting transfers between devices, swap(): return lax.ppermute(y, axis, [(i, i ^ step) for i in range(length)])  41.4 us
    ppermute x8, waiting for transfers between devices, swap(): return lax.ppermute(y, axis, [(i, i ^ step) for i in range(length)])  35.7 us
    unnamed x8, local copies, waits for them, and re-layouts  13.8 us
    ppermute x2, starting transfers between devices, passed_along(): return lax.ppermute(x, axis, pairs)  3.31 us
  transfers between devices with their start and end apart: 10, of which 9 were waited for; matrix products, arithmetic and copies ran while one was open for 5% of the time, Pallas kernels for 0%

profile of v1, /device:TPU:0, one launch (start us, length us, event | category | flops | bytes accessed | tf_op | source)
XLA Modules:
  0.0 143.4 jit_solution(14132581533321217572)
XLA Ops:
  0.6 2.5 %copy.22 = bf16[256,2,2048]{2,0,1:T(8,128)(2,1)S(1)} copy(bf16[256,2,2048]{2,1,0:T(2,128)(2,1)} %param.13) | data formatting | bytes 4194304 | tf_op args[0]
  3.1 0.0 copy-start
  3.1 1.3 collective-permute-start
  5.1 3.1 %copy.21 = f32[4,256,2,256]{3,1,2,0:T(8,128)} copy(f32[4,256,2,256]{3,2,1,0:T(2,128)} %param.14) | data formatting | bytes 4194304 | tf_op args[1]
  8.2 1.1 collective-permute-done.rim_hbm
  9.3 42.6 %step.1 = (f32[2,256,2048]{2,1,0:T(8,128)}, bf16[2,256,2048]{2,1,0:T(8,128)(2,1)}, f32[4,2,256,256]{3,2,1,0:T(8,128)}, f32[2,6]{1,0:T(2,128)}) custom-call(s32[1]{0:T(128)S(6)} %copy.23.count_ref, s32[6]{0:T(128)} %top_ref.1, s32[6]{0:T(128)} %left_ref.1, s32[6]{0:T(128)} %code_ref.1, bf16[2,256,2048]{2,1,0:T(8,128)(2,1)} %bitcast.14, ...), custom_call_target="tpu_custom_call" | custom-call | tf_op jit(solution)/shard_map/step/pallas_call | solution.py:234
  51.9 1.3 dynamic-slice_convert_fusion
  53.2 5.5 %collective-permute-start.2 = (bf16[8,128,256]{2,1,0:T(8,128)(2,1)S(1)}, bf16[8,128,256]{2,1,0:T(8,128)(2,1)S(1)}, u32[]{:S(2)}, u32[]{:S(2)}) collective-permute-start(bf16[8,128,256]{2,1,0:T(8,128)(2,1)S(1)} %dynamic-slice_convert_fusion), channel_id=1, source_target_pairs={{0,1},{1,0},{2,3},{3,2},{4,5},{5,4},{6,7},{7,6},{8,9},{9,8},{10,11... | collective-permute-start | bytes 1572872 | tf_op jit(solution)/shard_map/ppermute | solution.py:32
  58.6 1.5 %collective-permute-done.2 = bf16[8,128,256]{2,1,0:T(8,128)(2,1)S(1)} collective-permute-done((bf16[8,128,256]{2,1,0:T(8,128)(2,1)S(1)}, bf16[8,128,256]{2,1,0:T(8,128)(2,1)S(1)}, u32[]{:S(2)}, u32[]{:S(2)}) %collective-permute-start.2) | collective-permute-done | bytes 524320 | tf_op jit(solution)/shard_map/ppermute | solution.py:32
  60.2 1.3 convert_add_fusion
  61.6 19.7 %collective-permute-start.3 = (bf16[4,128,256]{2,1,0:T(8,128)(2,1)S(1)}, bf16[4,128,256]{2,1,0:T(8,128)(2,1)S(1)}, u32[]{:S(2)}, u32[]{:S(2)}) collective-permute-start(bf16[4,128,256]{2,1,0:T(8,128)(2,1)S(1)} %dynamic-slice_convert_fusion.1), channel_id=1, source_target_pairs={{0,2},{1,3},{2,0},{3,1},{4,6},{5,7},{6,4},{7,5},{8,10},{9,11},{10,... | collective-permute-start | bytes 786440 | tf_op jit(solution)/shard_map/ppermute | solution.py:32
  81.2 6.8 %collective-permute-done.3 = bf16[4,128,256]{2,1,0:T(8,128)(2,1)S(1)} collective-permute-done((bf16[4,128,256]{2,1,0:T(8,128)(2,1)S(1)}, bf16[4,128,256]{2,1,0:T(8,128)(2,1)S(1)}, u32[]{:S(2)}, u32[]{:S(2)}) %collective-permute-start.3) | collective-permute-done | bytes 262176 | tf_op jit(solution)/shard_map/ppermute | solution.py:32
  88.1 0.1 convert_add_fusion.1
  88.1 0.1 collective-permute-start.4
  88.3 2.0 %collective-permute-start.1 = (bf16[2,256,2048]{2,1,0:T(8,128)(2,1)}, bf16[2,256,2048]{2,1,0:T(8,128)(2,1)S(1)}, u32[]{:S(2)}, u32[]{:S(2)}) collective-permute-start(bf16[2,256,2048]{2,1,0:T(8,128)(2,1)} %get-tuple-element.28), channel_id=1, source_target_pairs={{0,1},{1,2},{2,3},{3,4},{4,5},{5,6},{6,7},{7,8},{8,9},{9,10},{10,1... | collective-permute-start | bytes 6291464 | tf_op jit(solution)/shard_map/ppermute | solution.py:19
  90.3 3.1 %collective-permute-done.4 = bf16[2,128,256]{2,1,0:T(8,128)(2,1)S(1)} collective-permute-done((bf16[2,128,256]{2,1,0:T(8,128)(2,1)S(1)}, bf16[2,128,256]{2,1,0:T(8,128)(2,1)S(1)}, u32[]{:S(2)}, u32[]{:S(2)}) %collective-permute-start.4) | collective-permute-done | bytes 131104 | tf_op jit(solution)/shard_map/ppermute | solution.py:32
  93.5 0.1 collective-permute-start.5
  93.6 5.8 %collective-permute-done.5 = bf16[1,128,256]{2,1,0:T(8,128)(2,1)S(1)} collective-permute-done((bf16[1,128,256]{2,1,0:T(8,128)(2,1)S(1)}, bf16[1,128,256]{2,1,0:T(8,128)(2,1)S(1)}, u32[]{:S(2)}, u32[]{:S(2)}) %collective-permute-start.5) | collective-permute-done | bytes 65568 | tf_op jit(solution)/shard_map/ppermute | solution.py:32
  99.4 0.1 collective-permute-start.6
  99.4 5.3 %collective-permute-done.6 = bf16[1,128,256]{2,1,0:T(8,128)(2,1)S(1)} collective-permute-done((bf16[1,128,256]{2,1,0:T(8,128)(2,1)S(1)}, bf16[1,128,256]{2,1,0:T(8,128)(2,1)S(1)}, u32[]{:S(2)}, u32[]{:S(2)}) %collective-permute-start.6) | collective-permute-done | bytes 65568 | tf_op jit(solution)/shard_map/ppermute | solution.py:32
  104.7 0.1 collective-permute-start.7
  104.8 4.9 %collective-permute-done.7 = bf16[2,128,256]{2,1,0:T(8,128)(2,1)S(1)} collective-permute-done((bf16[2,128,256]{2,1,0:T(8,128)(2,1)S(1)}, bf16[2,128,256]{2,1,0:T(8,128)(2,1)S(1)}, u32[]{:S(2)}, u32[]{:S(2)}) %collective-permute-start.7) | collective-permute-done | bytes 131104 | tf_op jit(solution)/shard_map/ppermute | solution.py:32
  109.8 1.2 collective-permute-start.8
  111.0 6.7 %collective-permute-done.8 = bf16[4,128,256]{2,1,0:T(8,128)(2,1)S(1)} collective-permute-done((bf16[4,128,256]{2,1,0:T(8,128)(2,1)S(1)}, bf16[4,128,256]{2,1,0:T(8,128)(2,1)S(1)}, u32[]{:S(2)}, u32[]{:S(2)}) %collective-permute-start.8) | collective-permute-done | bytes 262176 | tf_op jit(solution)/shard_map/ppermute | solution.py:32
  117.7 0.1 maximum_select_fusion.1
  117.8 14.8 %collective-permute-start.9 = (bf16[8,128,256]{2,1,0:T(8,128)(2,1)S(1)}, bf16[8,128,256]{2,1,0:T(8,128)(2,1)S(1)}, u32[]{:S(2)}, u32[]{:S(2)}) collective-permute-start(bf16[8,128,256]{2,1,0:T(8,128)(2,1)S(1)} %maximum_select_fusion.1), channel_id=1, source_target_pairs={{0,1},{1,0},{2,3},{3,2},{4,5},{5,4},{6,7},{7,6},{8,9},{9,8},{10,11... | collective-permute-start | bytes 1572872 | tf_op jit(solution)/shard_map/ppermute | solution.py:32
  132.6 1.5 %collective-permute-done.9 = bf16[8,128,256]{2,1,0:T(8,128)(2,1)S(1)} collective-permute-done((bf16[8,128,256]{2,1,0:T(8,128)(2,1)S(1)}, bf16[8,128,256]{2,1,0:T(8,128)(2,1)S(1)}, u32[]{:S(2)}, u32[]{:S(2)}) %collective-permute-start.9) | collective-permute-done | bytes 524320 | tf_op jit(solution)/shard_map/ppermute | solution.py:32
  134.2 0.2 maximum_select_fusion
  134.3 0.2 convert_bitcast_fusion
  134.5 2.9 %copy.18 = f32[4,256,2,256]{3,2,1,0:T(2,128)} copy(f32[4,256,2,256]{3,1,2,0:T(8,128)S(1)} %convert_bitcast_fusion) | data formatting | bytes 4194304
  137.5 0.6 add_bitcast_fusion
  138.1 5.2 %copy.17 = f32[256,2,2048]{2,1,0:T(2,128)} copy(f32[256,2,2048]{2,0,1:T(8,128)S(1)} %add_bitcast_fusion) | data formatting | bytes 8388608
  (11 shorter events, 0.2 us)
Async XLA Ops:
  3.1 5.1 %copy-start = (bf16[256,2,2048]{2,0,1:T(8,128)(2,1)}, bf16[256,2,2048]{2,0,1:T(8,128)(2,1)S(1)}, u32[]{:S(2)}) copy-start(bf16[256,2,2048]{2,0,1:T(8,128)(2,1)S(1)} %copy.22) | copy-start | bytes 6291460
  3.1 6.2 %collective-permute-start = (bf16[2,256,2048]{2,1,0:T(8,128)(2,1)S(1)}, bf16[2,256,2048]{2,1,0:T(8,128)(2,1)}, u32[]{:S(2)}, u32[]{:S(2)}) collective-permute-start(bf16[2,256,2048]{2,1,0:T(8,128)(2,1)S(1)} %bitcast.13), channel_id=1, source_target_pairs={{1,0},{2,1},{3,2},{4,3},{5,4},{6,5},{7,6},{8,7},{9,8},{10,9},{11,1... | collective-permute-start | bytes 6291464 | tf_op jit(solution)/shard_map/ppermute | solution.py:19
  53.2 7.0 %collective-permute-start.2 = (bf16[8,128,256]{2,1,0:T(8,128)(2,1)S(1)}, bf16[8,128,256]{2,1,0:T(8,128)(2,1)S(1)}, u32[]{:S(2)}, u32[]{:S(2)}) collective-permute-start(bf16[8,128,256]{2,1,0:T(8,128)(2,1)S(1)} %dynamic-slice_convert_fusion), channel_id=1, source_target_pairs={{0,1},{1,0},{2,3},{3,2},{4,5},{5,4},{6,7},{7,6},{8,9},{9,8},{10,11... | collective-permute-start | bytes 1572872 | tf_op jit(solution)/shard_map/ppermute | solution.py:32
  61.6 26.5 %collective-permute-start.3 = (bf16[4,128,256]{2,1,0:T(8,128)(2,1)S(1)}, bf16[4,128,256]{2,1,0:T(8,128)(2,1)S(1)}, u32[]{:S(2)}, u32[]{:S(2)}) collective-permute-start(bf16[4,128,256]{2,1,0:T(8,128)(2,1)S(1)} %dynamic-slice_convert_fusion.1), channel_id=1, source_target_pairs={{0,2},{1,3},{2,0},{3,1},{4,6},{5,7},{6,4},{7,5},{8,10},{9,11},{10,... | collective-permute-start | bytes 786440 | tf_op jit(solution)/shard_map/ppermute | solution.py:32
  88.1 5.3 %collective-permute-start.4 = (bf16[2,128,256]{2,1,0:T(8,128)(2,1)S(1)}, bf16[2,128,256]{2,1,0:T(8,128)(2,1)S(1)}, u32[]{:S(2)}, u32[]{:S(2)}) collective-permute-start(bf16[2,128,256]{2,1,0:T(8,128)(2,1)S(1)} %dynamic-slice_convert_fusion.2), channel_id=1, source_target_pairs={{0,4},{1,5},{2,6},{3,7},{4,0},{5,1},{6,2},{7,3},{8,12},{9,13},{10,... | collective-permute-start | bytes 393224 | tf_op jit(solution)/shard_map/ppermute | solution.py:32
  88.3 49.2 %collective-permute-start.1 = (bf16[2,256,2048]{2,1,0:T(8,128)(2,1)}, bf16[2,256,2048]{2,1,0:T(8,128)(2,1)S(1)}, u32[]{:S(2)}, u32[]{:S(2)}) collective-permute-start(bf16[2,256,2048]{2,1,0:T(8,128)(2,1)} %get-tuple-element.28), channel_id=1, source_target_pairs={{0,1},{1,2},{2,3},{3,4},{4,5},{5,6},{6,7},{7,8},{8,9},{9,10},{10,1... | collective-permute-start | bytes 6291464 | tf_op jit(solution)/shard_map/ppermute | solution.py:19
  93.5 5.9 %collective-permute-start.5 = (bf16[1,128,256]{2,1,0:T(8,128)(2,1)S(1)}, bf16[1,128,256]{2,1,0:T(8,128)(2,1)S(1)}, u32[]{:S(2)}, u32[]{:S(2)}) collective-permute-start(bf16[1,128,256]{2,1,0:T(8,128)(2,1)S(1)} %dynamic-slice_convert_fusion.3), channel_id=1, source_target_pairs={{0,8},{1,9},{2,10},{3,11},{4,12},{5,13},{6,14},{7,15},{8,0},{9,1},... | collective-permute-start | bytes 196616 | tf_op jit(solution)/shard_map/ppermute | solution.py:32
  99.4 5.4 %collective-permute-start.6 = (bf16[1,128,256]{2,1,0:T(8,128)(2,1)S(1)}, bf16[1,128,256]{2,1,0:T(8,128)(2,1)S(1)}, u32[]{:S(2)}, u32[]{:S(2)}) collective-permute-start(bf16[1,128,256]{2,1,0:T(8,128)(2,1)S(1)} %add_convert_fusion), channel_id=1, source_target_pairs={{0,8},{1,9},{2,10},{3,11},{4,12},{5,13},{6,14},{7,15},{8,0},{9,1},... | collective-permute-start | bytes 196616 | tf_op jit(solution)/shard_map/ppermute | solution.py:32
  104.7 5.0 %collective-permute-start.7 = (bf16[2,128,256]{2,1,0:T(8,128)(2,1)S(1)}, bf16[2,128,256]{2,1,0:T(8,128)(2,1)S(1)}, u32[]{:S(2)}, u32[]{:S(2)}) collective-permute-start(bf16[2,128,256]{2,1,0:T(8,128)(2,1)S(1)} %maximum_select_fusion.3), channel_id=1, source_target_pairs={{0,4},{1,5},{2,6},{3,7},{4,0},{5,1},{6,2},{7,3},{8,12},{9,13},{10,... | collective-permute-start | bytes 393224 | tf_op jit(solution)/shard_map/ppermute | solution.py:32
  109.8 7.9 %collective-permute-start.8 = (bf16[4,128,256]{2,1,0:T(8,128)(2,1)S(1)}, bf16[4,128,256]{2,1,0:T(8,128)(2,1)S(1)}, u32[]{:S(2)}, u32[]{:S(2)}) collective-permute-start(bf16[4,128,256]{2,1,0:T(8,128)(2,1)S(1)} %maximum_select_fusion.2), channel_id=1, source_target_pairs={{0,2},{1,3},{2,0},{3,1},{4,6},{5,7},{6,4},{7,5},{8,10},{9,11},{10,... | collective-permute-start | bytes 786440 | tf_op jit(solution)/shard_map/ppermute | solution.py:32
  117.8 16.4 %collective-permute-start.9 = (bf16[8,128,256]{2,1,0:T(8,128)(2,1)S(1)}, bf16[8,128,256]{2,1,0:T(8,128)(2,1)S(1)}, u32[]{:S(2)}, u32[]{:S(2)}) collective-permute-start(bf16[8,128,256]{2,1,0:T(8,128)(2,1)S(1)} %maximum_select_fusion.1), channel_id=1, source_target_pairs={{0,1},{1,0},{2,3},{3,2},{4,5},{5,4},{6,7},{7,6},{8,9},{9,8},{10,11... | collective-permute-start | bytes 1572872 | tf_op jit(solution)/shard_map/ppermute | solution.py:32
  134.5 3.0 %copy-start.1 = (f32[2,256,2048]{2,1,0:T(8,128)S(1)}, f32[2,256,2048]{2,1,0:T(8,128)}, u32[]{:S(2)}) copy-start(f32[2,256,2048]{2,1,0:T(8,128)} %get-tuple-element.27) | copy-start | bytes 12582916
